TPU v7x, 128 devices: a whole 4x4x4 slice. The times are simulated.
128 devices in a mesh: section: 16 (over z_lo, y, core), tensor: 8 (over x, z_hi).
Axes of the slice: x: 4, y: 4, z: 4 (z_hi: 2, z_lo: 2; z = z_hi * 2 + z_lo), core: 2. Of those that a mesh axis runs over, the one named last changes fastest.
Arguments:
- inflow: bfloat16 [16, 512, 12288], P('section', 'tensor'), may hold values from -60 to 60
- fresh: bfloat16 [512, 12288], P('tensor'), may hold values from -60 to 60
- stash_held: bfloat16 [16, 512, 12288], P('section', 'tensor'), may hold values from -60 to 60
- grad_in: bfloat16 [16, 512, 12288], P('section', 'tensor'), may hold values from -6 to 6
- query_gain: float32 [16, 12288], P('section', 'tensor'), may hold values from -3 to 3
- key_gain: float32 [16, 12288], P('section', 'tensor'), may hold values from -3 to 3
- value_gain: float32 [16, 12288], P('section', 'tensor'), may hold values from -4 to 4
Outputs:
- first_out: bfloat16 [16, 512, 12288], P('section', 'tensor')
- second_out: bfloat16 [16, 512, 12288], P('section', 'tensor')
- evicted: bfloat16 [16, 512, 12288], P('section', 'tensor')
- grad_out: bfloat16 [16, 512, 12288], P('section', 'tensor')
All inputs are finite; a program needn't handle non-finite values.
Results may differ from a plain program's by a relative error of at most 0.0068.
Values may be sent and summed in bfloat16 or wider, within the bound.
No kernel may reach another device: no remote copies, remote signals or barrier semaphores. Data moves between devices by JAX's collectives and lax.ppermute only.
A program may use at most 128 MiB of HBM per device.

v0:
```python
import jax
import jax.numpy as jnp
from jax import lax
from jax.sharding import PartitionSpec as P

HDIM = 128
epsilon = 1e-05
masked_score = -1e30


def from_partner(value, axis, distance):
    mask = 2**distance
    pairs = [(source, source ^ mask) for source in range(lax.axis_size(axis))]
    return lax.ppermute(value, axis, pairs)


def from_behind(x, axis, by):
    peers = lax.axis_size(axis)
    pairs = [(i, i + by) for i in range(peers) if 0 <= i + by < peers]
    return lax.ppermute(x, axis, pairs)


def normalize(tokens_in):
    values = tokens_in.astype(jnp.float32)
    factor = lax.rsqrt(jnp.mean(values * values, axis=-1, keepdims=True) + epsilon)
    return (values * factor, factor)


def heads_of(normed, feature_gain):
    scaled = (normed.astype(jnp.float32) * feature_gain).astype(jnp.bfloat16)
    return scaled.reshape(scaled.shape[0], -1, HDIM)


def softmax_causal(queries, key_heads):
    scores = jnp.einsum("ihd,jhd->hij", queries, key_heads, preferred_element_type=jnp.float32)
    scores = scores * HDIM ** (-0.5)
    length = queries.shape[0]
    row_index = lax.broadcasted_iota(jnp.int32, (length, length), 0)
    col_index = lax.broadcasted_iota(jnp.int32, (length, length), 1)
    scores = jnp.where(row_index >= col_index, scores, masked_score)
    largest = jnp.max(scores, axis=-1, keepdims=True)
    weights = jnp.exp(scores - largest)
    return weights / jnp.sum(weights, axis=-1, keepdims=True)


def forward(tokens_in, query_gain, key_gain, value_gain):
    scaled, factor = normalize(tokens_in)
    normed = scaled.astype(jnp.bfloat16)
    spread = lax.all_to_all(normed, "tensor", split_axis=1, concat_axis=0, tiled=True)
    queries = heads_of(spread, query_gain)
    key_heads = heads_of(spread, key_gain)
    value_heads = heads_of(spread, value_gain)
    weights = softmax_causal(queries, key_heads).astype(jnp.bfloat16)
    mixed_out = jnp.einsum("hij,jhd->ihd", weights, value_heads, preferred_element_type=jnp.float32)
    mixed_out = mixed_out.astype(jnp.bfloat16).reshape(spread.shape)
    merged = lax.all_to_all(mixed_out, "tensor", split_axis=0, concat_axis=1, tiled=True)
    return (tokens_in.astype(jnp.float32) + merged.astype(jnp.float32)).astype(jnp.bfloat16)


def backward(stash_rows, grad_rows, query_gain, key_gain, value_gain):
    scaled, factor = normalize(stash_rows)
    normed = scaled.astype(jnp.bfloat16)
    spread, grad_heads = (
        lax.all_to_all(normed, "tensor", split_axis=1, concat_axis=0, tiled=True),
        lax.all_to_all(grad_rows, "tensor", split_axis=1, concat_axis=0, tiled=True),
    )
    queries = heads_of(spread, query_gain)
    key_heads = heads_of(spread, key_gain)
    value_heads = heads_of(spread, value_gain)
    cotangent = grad_heads.reshape(grad_heads.shape[0], -1, HDIM)
    weights = softmax_causal(queries, key_heads)
    weights_low = weights.astype(jnp.bfloat16)
    value_grad = jnp.einsum(
        "hij,ihd->jhd", weights_low, cotangent, preferred_element_type=jnp.float32
    )
    prob_grad = jnp.einsum(
        "ihd,jhd->hij", cotangent, value_heads, preferred_element_type=jnp.float32
    )
    score_grad = weights * (prob_grad - jnp.sum(prob_grad * weights, axis=-1, keepdims=True))
    score_low = score_grad.astype(jnp.bfloat16)
    query_grad = jnp.einsum(
        "hij,jhd->ihd", score_low, key_heads, preferred_element_type=jnp.float32
    )
    key_grad = jnp.einsum("hij,ihd->jhd", score_low, queries, preferred_element_type=jnp.float32)
    query_grad = query_grad * HDIM ** (-0.5)
    key_grad = key_grad * HDIM ** (-0.5)
    head_shape = spread.shape
    normed_grad = (
        query_grad.reshape(head_shape) * query_gain + key_grad.reshape(head_shape) * key_gain
    )
    normed_grad = (normed_grad + value_grad.reshape(head_shape) * value_gain).astype(jnp.bfloat16)
    returned = lax.all_to_all(
        normed_grad, "tensor", split_axis=0, concat_axis=1, tiled=True
    ).astype(jnp.float32)
    inner = jnp.mean(returned * scaled, axis=-1, keepdims=True)
    return (grad_rows.astype(jnp.float32) + factor * (returned - scaled * inner)).astype(
        jnp.bfloat16
    )


def bit_order(count):
    numbers = list(range(count))
    return numbers


def evict_chain(payload, numbers):
    for bit_number in numbers:
        payload = from_partner(payload, "section", bit_number)
    return payload


def reload_chain(payload, numbers):
    for bit_number in numbers:
        payload = from_partner(payload, "section", bit_number)
    return payload


def per_device(inflow, fresh, stash_held, grad_in, query_gain, key_gain, value_gain):
    numbers = bit_order(lax.axis_size("section").bit_length() - 1)
    gain_query = query_gain[0]
    gain_key = key_gain[0]
    gain_value = value_gain[0]
    first_out = forward(inflow[0], gain_query, gain_key, gain_value)
    moved = from_behind(first_out, "section", 1)
    second_in = jnp.where(lax.axis_index("section") == 0, fresh, moved)
    second_out = forward(second_in, gain_query, gain_key, gain_value)
    evicted = evict_chain(inflow[0], numbers)
    stash_rows = reload_chain(stash_held[0], numbers)
    grad_out = backward(stash_rows, grad_in[0], gain_query, gain_key, gain_value)
    return (first_out[None], second_out[None], evicted[None], grad_out[None])


def solution(mesh):
    placed = (
        P("section", "tensor", None),
        P("tensor", None),
        P("section", "tensor", None),
        P("section", "tensor", None),
        P("section", "tensor"),
        P("section", "tensor"),
        P("section", "tensor"),
    )
    return jax.shard_map(
        per_device,
        mesh=mesh,
        in_specs=placed,
        out_specs=(
            P("section", "tensor", None),
            P("section", "tensor", None),
            P("section", "tensor", None),
            P("section", "tensor", None),
        ),
        check_vma=False,
    )
```

profile of v0, /device:TPU:0, one launch (start us, length us, event | category | flops | bytes accessed | tf_op | source)
XLA Modules:
  0.0 462.2 jit_solution(15312056894646589805)
XLA Ops:
  0.7 3.6 collective-permute-done.5
  6.0 34.7 %collective-permute-done.6 = bf16[64,12288]{1,0:T(8,128)(2,1)S(1)} collective-permute-done((bf16[64,12288]{1,0:T(8,128)(2,1)S(1)}, bf16[64,12288]{1,0:T(8,128)(2,1)S(1)}, u32[]{:S(2)}, u32[]{:S(2)}) %collective-permute-start.6) | collective-permute-done | bytes 1572896 | tf_op jit(solution)/shard_map/ppermute | solution.py:14
  40.8 3.3 collective-permute-start.7
  44.8 34.9 %collective-permute-done.7 = bf16[64,12288]{1,0:T(8,128)(2,1)} collective-permute-done((bf16[64,12288]{1,0:T(8,128)(2,1)S(1)}, bf16[64,12288]{1,0:T(8,128)(2,1)}, u32[]{:S(2)}, u32[]{:S(2)}) %collective-permute-start.7) | collective-permute-done | bytes 1572896 | tf_op jit(solution)/shard_map/ppermute | solution.py:14
  79.6 2.0 collective-permute-start.8
  81.7 1.9 copy.95
  85.2 7.3 %all-to-all-start.5 = ((bf16[64,8,1536]{2,0,1:T(8,128)(2,1)}), bf16[64,8,1536]{2,0,1:T(8,128)(2,1)}, u32[]{:S(2)}, u32[]{:S(2)}) async-start(bf16[64,8,1536]{2,0,1:T(8,128)(2,1)} %copy.73), calls=%async_computation.5 | async-start | bytes 3145728 | tf_op jit(solution)/shard_map/all_to_all | solution.py:65
  93.5 2.9 fusion.36
  96.4 15.8 %collective-permute-done.2 = bf16[64,12288]{1,0:T(8,128)(2,1)} collective-permute-done((bf16[64,12288]{1,0:T(8,128)(2,1)}, bf16[64,12288]{1,0:T(8,128)(2,1)}, u32[]{:S(2)}, u32[]{:S(2)}) %collective-permute-start.2) | collective-permute-done | bytes 1572896 | tf_op jit(solution)/shard_map/ppermute | solution.py:14
  112.1 1.8 collective-permute-start.3
  114.0 14.0 %collective-permute-done.8 = bf16[64,12288]{1,0:T(8,128)(2,1)S(1)} collective-permute-done((bf16[64,12288]{1,0:T(8,128)(2,1)}, bf16[64,12288]{1,0:T(8,128)(2,1)S(1)}, u32[]{:S(2)}, u32[]{:S(2)}) %collective-permute-start.8) | collective-permute-done | bytes 1572896 | tf_op jit(solution)/shard_map/ppermute | solution.py:14
  128.3 5.1 %all-to-all-done.5 = bf16[64,8,1536]{2,0,1:T(8,128)(2,1)} async-done(((bf16[64,8,1536]{2,0,1:T(8,128)(2,1)}), bf16[64,8,1536]{2,0,1:T(8,128)(2,1)}, u32[]{:S(2)}, u32[]{:S(2)}) %all-to-all-start.5) | async-done | bytes 1572896 | tf_op jit(solution)/shard_map/all_to_all | solution.py:65
  133.4 4.3 all-to-all-start
  139.4 17.0 %all-to-all-done = bf16[64,8,1536]{2,0,1:T(8,128)(2,1)} async-done(((bf16[64,8,1536]{2,0,1:T(8,128)(2,1)}), bf16[64,8,1536]{2,0,1:T(8,128)(2,1)}, u32[]{:S(2)}, u32[]{:S(2)}) %all-to-all-start) | async-done | bytes 1572896 | tf_op jit(solution)/shard_map/all_to_all | solution.py:49
  156.4 4.1 all-to-all-start.4
  160.7 4.0 reshape.197
  164.7 3.5 convert_bitcast_fusion.6
  168.2 4.6 %reshape.202 = f32[512,12,128]{2,1,0:T(8,128)} reshape(f32[8,64,1536]{2,1,0:T(8,128)} %convert_bitcast_fusion.6) | data formatting | bytes 6291456 | tf_op jit(solution)/shard_map/convert_element_type | solution.py:30
  173.0 8.9 %all-to-all-done.4 = bf16[64,8,1536]{2,0,1:T(8,128)(2,1)S(1)} async-done(((bf16[64,8,1536]{2,0,1:T(8,128)(2,1)}), bf16[64,8,1536]{2,0,1:T(8,128)(2,1)S(1)}, u32[]{:S(2)}, u32[]{:S(2)}) %all-to-all-start.4) | async-done | bytes 1572896 | tf_op jit(solution)/shard_map/all_to_all | solution.py:64
  181.8 2.1 convert_bitcast_fusion.3
  184.0 4.6 %reshape.208 = f32[512,12,128]{2,1,0:T(8,128)} reshape(f32[8,64,1536]{2,1,0:T(8,128)} %convert_bitcast_fusion.3) | data formatting | bytes 6291456 | tf_op jit(solution)/shard_map/convert_element_type | solution.py:30
  188.6 7.1 %multiply_convert_fusion.8 = (bf16[512,12,128]{2,1,0:T(8,128)(2,1)}, bf16[512,12,128]{2,1,0:T(8,128)(2,1)}, bf16[512,12,128]{2,1,0:T(8,128)(2,1)}, bf16[512,12,1...) fusion(f32[512,12,128]{2,1,0:T(8,128)} %reshape.202, f32[12,128]{1,0:T(8,128)S(1)} %bitcast.93, ...), kind=kLoop, calls=%fused_computation.44 | loop fusion | flops 9437184 | bytes 15747072 | tf_op jit(solution)/shard_map/convert_element_type | solution.py:30
  195.7 3.3 copy.76
  199.0 4.3 copy.79
  203.3 4.1 fusion.51
  207.3 8.2 %fusion.70 = (f32[12,512]{1,0:T(8,128)S(1)}, f32[12,512,512]{1,2,0:T(8,128)}) fusion(f32[12,512,512]{1,2,0:T(8,128)S(1)} %fusion.51, pred[512,512]{0,1:T(8,128)(4,1)S(1)} %iota_compare_fusion), kind=kOutput, calls=%fused_computation.110 | output fusion | flops 18874880 | bytes 25452544 | tf_op jit(solution)/shard_map/sub | solution.py:42
  215.5 7.9 %fusion.54 = bf16[512,12,128]{0,2,1:T(8,128)(2,1)} fusion(f32[12,512,512]{1,2,0:T(8,128)} %get-tuple-element.21, f32[12,512]{1,0:T(8,128)S(1)} %get-tuple-element.20, bf16[512,12,128]{2,1,0:T(8,128)(2,1)} %get-tuple-element.12), kind=kOutput, calls=%fused_computation.94 | convolution fusion | flops 812384256 | bytes 15753216 | tf_op jit(solution)/shard_map/hij,jhd->ihd/dot_general | solution.py:54
  223.5 4.4 copy.60
  227.9 4.0 all_to_all.34
  231.8 4.5 all-to-all-start.1
  236.3 10.6 %fusion.72 = (f32[12,512]{1,0:T(8,128)S(1)}, f32[12,512,512]{1,2,0:T(8,128)}) fusion(pred[512,512]{0,1:T(8,128)(4,1)S(1)} %iota_compare_fusion, bf16[512,12,128]{0,2,1:T(8,128)(2,1)} %copy.79, bf16[512,12,128]{0,2,1:T(8,128)(2,1)S(1)} %copy.76), kind=kOutput, calls=%fused_computation.112 | convolution fusion | flops 817889792 | bytes 16015360 | tf_op jit(solution)/shard_map/sub | solution.py:42
  246.9 8.8 %fusion.37 = f32[512,12,128]{2,0,1:T(8,128)} fusion(bf16[512,12,128]{2,1,0:T(8,128)(2,1)} %reshape.197, f32[12,512,512]{1,2,0:T(8,128)} %get-tuple-element.25, f32[12,512]{1,0:T(8,128)S(1)} %get-tuple-element.24), kind=kOutput, calls=%fused_computation.76 | convolution fusion | flops 811597824 | bytes 17326080 | tf_op jit(solution)/shard_map/hij,ihd->jhd/dot_general | solution.py:73
  256.8 9.5 %fusion.3 = (f32[12,512]{1,0:T(8,128)S(1)}, f32[12,512,512]{2,1,0:T(8,128)}) fusion(f32[12,512,512]{1,2,0:T(8,128)S(1)} %copy-done.8, f32[12,512]{1,0:T(8,128)S(1)} %get-tuple-element.24, bf16[512,12,128]{2,1,0:T(8,128)(2,1)} %reshape.197, bf16[512,12,128]{2,1,0:T(8,128)(2,1)} %get-tuple-element.19), kind=kOutput, calls=%fused_computation.5 | convolution fusion | flops 814737408 | bytes 28360704 | tf_op jit(solution)/shard_map/ihd,jhd->hij/dot_general | solution.py:76
  266.3 7.2 %fusion.5 = bf16[12,512,512]{1,2,0:T(8,128)(2,1)S(1)} fusion(f32[12,512,512]{2,1,0:T(8,128)} %get-tuple-element.27, f32[12,512]{1,0:T(8,128)S(1)} %get-tuple-element.26, f32[12,512,512]{1,2,0:T(8,128)S(1)} %copy-done.8, f32[12,512]{1,0:T(8,128)S(1)} %get-tuple-element.24), kind=kLoop, calls=%fused_computation.7 | loop fusion | flops 12582912 | bytes 31506432 | tf_op jit(solution)/shard_map/convert_element_type | solution.py:80
  273.5 2.7 multiply_bitcast_fusion.1
  277.7 3.9 copy.83
  281.6 4.7 %reshape.200 = f32[8,64,1536]{2,1,0:T(8,128)} reshape(f32[512,12,128]{2,1,0:T(8,128)} %copy.83) | data formatting | bytes 6291456 | tf_op jit(solution)/shard_map/reshape | solution.py:91
  286.3 5.1 %copy.78 = f32[512,12,128]{2,1,0:T(8,128)} copy(f32[512,12,128]{0,2,1:T(8,128)} %multiply_bitcast_fusion.1) | data formatting | bytes 6291456 | tf_op jit(solution)/shard_map/mul | solution.py:85
  291.4 4.8 %reshape.198 = f32[8,64,1536]{2,1,0:T(8,128)} reshape(f32[512,12,128]{2,1,0:T(8,128)} %copy.78) | data formatting | bytes 6291456 | tf_op jit(solution)/shard_map/reshape | solution.py:89
  296.2 6.6 %multiply_bitcast_fusion = f32[512,12,128]{0,2,1:T(8,128)} fusion(bf16[512,12,128]{0,2,1:T(8,128)(2,1)S(1)} %copy-done.9, bf16[12,512,512]{1,2,0:T(8,128)(2,1)} %copy-done), kind=kOutput, calls=%fused_computation.73 | convolution fusion | flops 806092800 | bytes 11010048 | tf_op jit(solution)/shard_map/hij,ihd->jhd/dot_general | solution.py:84
  302.8 5.1 %copy.81 = f32[512,12,128]{2,1,0:T(8,128)} copy(f32[512,12,128]{0,2,1:T(8,128)} %multiply_bitcast_fusion) | data formatting | bytes 6291456 | tf_op jit(solution)/shard_map/mul | solution.py:86
  307.9 4.7 %reshape.199 = f32[8,64,1536]{2,1,0:T(8,128)} reshape(f32[512,12,128]{2,1,0:T(8,128)} %copy.81) | data formatting | bytes 6291456 | tf_op jit(solution)/shard_map/reshape | solution.py:89
  312.6 6.1 %add_convert_fusion = bf16[8,64,1536]{2,1,0:T(8,128)(2,1)} fusion(f32[8,64,1536]{2,1,0:T(8,128)} %reshape.200, f32[8,64,1536]{2,1,0:T(8,128)} %reshape.199, f32[8,64,1536]{2,1,0:T(8,128)} %reshape.198, f32[1536]{0:T(1024)S(1)} %reduce, f32[1536]{0:T(1024)S(1)} %reduce.2, f32[1536]{0:T(1024)S(1)} %reduce.1), kind=kLoop, calls=%fused_computation.72 | loop fusion | flops 4718592 | bytes 11028480 | tf_op jit(solution)/shard_map/convert_element_type | solution.py:91
  318.7 7.2 %all-to-all-start.6 = ((bf16[8,64,1536]{2,1,0:T(8,128)(2,1)}), bf16[8,64,1536]{2,1,0:T(8,128)(2,1)S(1)}, u32[]{:S(2)}, u32[]{:S(2)}) async-start(bf16[8,64,1536]{2,1,0:T(8,128)(2,1)} %add_convert_fusion), calls=%async_computation.6 | async-start | bytes 3145728 | tf_op jit(solution)/shard_map/all_to_all | solution.py:92
  325.9 3.5 convert_bitcast_fusion
  331.1 2.4 collective-permute-start
  333.6 28.7 %all-to-all-done.6 = bf16[8,64,1536]{2,1,0:T(8,128)(2,1)S(1)} async-done(((bf16[8,64,1536]{2,1,0:T(8,128)(2,1)}), bf16[8,64,1536]{2,1,0:T(8,128)(2,1)S(1)}, u32[]{:S(2)}, u32[]{:S(2)}) %all-to-all-start.6) | async-done | bytes 1572896 | tf_op jit(solution)/shard_map/all_to_all | solution.py:92
  367.2 4.5 all-to-all-start.2
  371.7 4.0 fusion.43
  375.7 1.8 copy.61
  377.5 1.9 reshape.203
  379.5 17.8 %all-to-all-done.2 = bf16[64,8,1536]{2,0,1:T(8,128)(2,1)} async-done(((bf16[64,8,1536]{2,0,1:T(8,128)(2,1)}), bf16[64,8,1536]{2,0,1:T(8,128)(2,1)}, u32[]{:S(2)}, u32[]{:S(2)}) %all-to-all-start.2) | async-done | bytes 1572896 | tf_op jit(solution)/shard_map/all_to_all | solution.py:49
  397.2 1.8 convert_bitcast_fusion.5
  399.0 2.2 reshape.205
  401.3 3.2 multiply_convert_fusion.5
  404.5 1.9 fusion.47
  406.4 8.2 %fusion.71 = (f32[12,512]{1,0:T(8,128)S(1)}, f32[12,512,512]{1,2,0:T(8,128)}) fusion(f32[12,512,512]{1,2,0:T(8,128)S(1)} %fusion.47, pred[512,512]{0,1:T(8,128)(4,1)S(1)} %iota_compare_fusion), kind=kOutput, calls=%fused_computation.111 | output fusion | flops 18874880 | bytes 25452544 | tf_op jit(solution)/shard_map/sub | solution.py:42
  414.6 6.1 %fusion.57 = bf16[512,12,128]{0,2,1:T(8,128)(2,1)S(1)} fusion(f32[12,512,512]{1,2,0:T(8,128)} %get-tuple-element.23, f32[12,512]{1,0:T(8,128)S(1)} %get-tuple-element.22, bf16[512,12,128]{2,1,0:T(8,128)(2,1)S(1)} %get-tuple-element.9), kind=kOutput, calls=%fused_computation.95 | convolution fusion | flops 812384256 | bytes 15753216 | tf_op jit(solution)/shard_map/hij,jhd->ihd/dot_general | solution.py:54
  420.7 3.0 copy.68
  423.7 4.1 all_to_all.73
  427.8 4.5 all-to-all-start.3
  432.3 3.3 add_convert_fusion.1
  435.6 20.6 %all-to-all-done.3 = bf16[8,64,1536]{2,1,0:T(8,128)(2,1)S(1)} async-done(((bf16[8,64,1536]{2,1,0:T(8,128)(2,1)}), bf16[8,64,1536]{2,1,0:T(8,128)(2,1)S(1)}, u32[]{:S(2)}, u32[]{:S(2)}) %all-to-all-start.3) | async-done | bytes 1572896 | tf_op jit(solution)/shard_map/all_to_all | solution.py:56
  459.4 2.7 copy.130
  (65 shorter events, 19.8 us)
Async XLA Ops:
  0.6 3.7 collective-permute-start.5
  4.3 36.4 %collective-permute-start.6 = (bf16[64,12288]{1,0:T(8,128)(2,1)S(1)}, bf16[64,12288]{1,0:T(8,128)(2,1)S(1)}, u32[]{:S(2)}, u32[]{:S(2)}) collective-permute-start(bf16[64,12288]{1,0:T(8,128)(2,1)S(1)} %collective-permute-done.5), channel_id=1, source_target_pairs={{0,16},{8,24},{16,0},{24,8},{32,48},{40,56},{48,32},{56,40},{64,80... | collective-permute-start | bytes 4718600 | tf_op jit(solution)/shard_map/ppermute | solution.py:14
  6.0 38.1 %collective-permute-start.1 = (bf16[64,12288]{1,0:T(8,128)(2,1)}, bf16[64,12288]{1,0:T(8,128)(2,1)}, u32[]{:S(2)}, u32[]{:S(2)}) collective-permute-start(bf16[64,12288]{1,0:T(8,128)(2,1)} %bitcast.79), channel_id=1, source_target_pairs={{0,8},{8,0},{16,24},{24,16},{32,40},{40,32},{48,56},{56,48},{64,72... | collective-permute-start | bytes 4718600 | tf_op jit(solution)/shard_map/ppermute | solution.py:14
  40.8 38.9 %collective-permute-start.7 = (bf16[64,12288]{1,0:T(8,128)(2,1)S(1)}, bf16[64,12288]{1,0:T(8,128)(2,1)}, u32[]{:S(2)}, u32[]{:S(2)}) collective-permute-start(bf16[64,12288]{1,0:T(8,128)(2,1)S(1)} %collective-permute-done.6), channel_id=1, source_target_pairs={{0,32},{8,40},{16,48},{24,56},{32,0},{40,8},{48,16},{56,24},{64,96... | collective-permute-start | bytes 4718600 | tf_op jit(solution)/shard_map/ppermute | solution.py:14
  44.1 68.0 %collective-permute-start.2 = (bf16[64,12288]{1,0:T(8,128)(2,1)}, bf16[64,12288]{1,0:T(8,128)(2,1)}, u32[]{:S(2)}, u32[]{:S(2)}) collective-permute-start(bf16[64,12288]{1,0:T(8,128)(2,1)} %collective-permute-done.1), channel_id=1, source_target_pairs={{0,16},{8,24},{16,0},{24,8},{32,48},{40,56},{48,32},{56,40},{64,80... | collective-permute-start | bytes 4718600 | tf_op jit(solution)/shard_map/ppermute | solution.py:14
  79.6 48.3 %collective-permute-start.8 = (bf16[64,12288]{1,0:T(8,128)(2,1)}, bf16[64,12288]{1,0:T(8,128)(2,1)S(1)}, u32[]{:S(2)}, u32[]{:S(2)}) collective-permute-start(bf16[64,12288]{1,0:T(8,128)(2,1)} %collective-permute-done.7), channel_id=1, source_target_pairs={{0,64},{8,72},{16,80},{24,88},{32,96},{40,104},{48,112},{56,120},{... | collective-permute-start | bytes 4718600 | tf_op jit(solution)/shard_map/ppermute | solution.py:14
  83.6 8.9 %copy-start.3 = (bf16[1,64,12288]{2,1,0:T(8,128)(2,1)S(1)}, bf16[1,64,12288]{2,1,0:T(8,128)(2,1)}, u32[]{:S(2)}) copy-start(bf16[1,64,12288]{2,1,0:T(8,128)(2,1)} %param.7) | copy-start | bytes 4718596
  85.2 48.2 %all-to-all-start.5 = ((bf16[64,8,1536]{2,0,1:T(8,128)(2,1)}), bf16[64,8,1536]{2,0,1:T(8,128)(2,1)}, u32[]{:S(2)}, u32[]{:S(2)}) async-start(bf16[64,8,1536]{2,0,1:T(8,128)(2,1)} %copy.73), calls=%async_computation.5 | async-start | bytes 3145728 | tf_op jit(solution)/shard_map/all_to_all | solution.py:65
  112.1 60.7 %collective-permute-start.3 = (bf16[64,12288]{1,0:T(8,128)(2,1)}, bf16[64,12288]{1,0:T(8,128)(2,1)}, u32[]{:S(2)}, u32[]{:S(2)}) collective-permute-start(bf16[64,12288]{1,0:T(8,128)(2,1)} %collective-permute-done.2), channel_id=1, source_target_pairs={{0,32},{8,40},{16,48},{24,56},{32,0},{40,8},{48,16},{56,24},{64,96... | collective-permute-start | bytes 4718600 | tf_op jit(solution)/shard_map/ppermute | solution.py:14
  127.9 10.2 %copy-start.1 = (bf16[64,12288]{1,0:T(8,128)(2,1)}, bf16[64,12288]{1,0:T(8,128)(2,1)S(1)}, u32[]{:S(2)}) copy-start(bf16[64,12288]{1,0:T(8,128)(2,1)S(1)} %collective-permute-done.8) | copy-start | bytes 4718596
  133.4 22.9 %all-to-all-start = ((bf16[64,8,1536]{2,0,1:T(8,128)(2,1)}), bf16[64,8,1536]{2,0,1:T(8,128)(2,1)}, u32[]{:S(2)}, u32[]{:S(2)}) async-start(bf16[64,8,1536]{2,0,1:T(8,128)(2,1)} %fusion.36), calls=%async_computation | async-start | bytes 3145728 | tf_op jit(solution)/shard_map/all_to_all | solution.py:49
  138.1 22.4 %copy-start.12 = (f32[1,1536]{1,0:T(1,128)S(1)}, f32[1,1536]{1,0:T(1,128)}, u32[]{:S(2)}) copy-start(f32[1,1536]{1,0:T(1,128)} %param.11) | copy-start | bytes 18436
  138.1 22.4 %copy-start.13 = (f32[1,1536]{1,0:T(1,128)S(1)}, f32[1,1536]{1,0:T(1,128)}, u32[]{:S(2)}) copy-start(f32[1,1536]{1,0:T(1,128)} %param.12) | copy-start | bytes 18436
  138.1 22.4 %copy-start.14 = (f32[1,1536]{1,0:T(1,128)S(1)}, f32[1,1536]{1,0:T(1,128)}, u32[]{:S(2)}) copy-start(f32[1,1536]{1,0:T(1,128)} %param.13) | copy-start | bytes 18436
  156.4 25.5 %all-to-all-start.4 = ((bf16[64,8,1536]{2,0,1:T(8,128)(2,1)}), bf16[64,8,1536]{2,0,1:T(8,128)(2,1)S(1)}, u32[]{:S(2)}, u32[]{:S(2)}) async-start(bf16[64,8,1536]{2,0,1:T(8,128)(2,1)} %bitcast.75), calls=%async_computation.4 | async-start | bytes 3145728 | tf_op jit(solution)/shard_map/all_to_all | solution.py:64
  172.8 160.8 %collective-permute-start.4 = (bf16[64,12288]{1,0:T(8,128)(2,1)}, bf16[64,12288]{1,0:T(8,128)(2,1)}, u32[]{:S(2)}, u32[]{:S(2)}) collective-permute-start(bf16[64,12288]{1,0:T(8,128)(2,1)} %collective-permute-done.3), channel_id=1, source_target_pairs={{0,64},{8,72},{16,80},{24,88},{32,96},{40,104},{48,112},{56,120},{... | collective-permute-start | bytes 4718600 | tf_op jit(solution)/shard_map/ppermute | solution.py:14
  231.8 86.9 %all-to-all-start.1 = ((bf16[8,64,1536]{2,1,0:T(8,128)(2,1)}), bf16[8,64,1536]{2,1,0:T(8,128)(2,1)}, u32[]{:S(2)}, u32[]{:S(2)}) async-start(bf16[8,64,1536]{2,1,0:T(8,128)(2,1)} %all_to_all.34), calls=%async_computation.1 | async-start | bytes 3145728 | tf_op jit(solution)/shard_map/all_to_all | solution.py:56
  246.9 9.9 %copy-start.8 = (f32[12,512,512]{1,2,0:T(8,128)S(1)}, f32[12,512,512]{1,2,0:T(8,128)}, u32[]{:S(2)}) copy-start(f32[12,512,512]{1,2,0:T(8,128)} %get-tuple-element.25) | copy-start | bytes 37748740
  273.5 4.2 copy-start
  273.5 4.2 copy-start.10
  291.4 4.8 %copy-start.9 = (bf16[512,12,128]{0,2,1:T(8,128)(2,1)S(1)}, bf16[512,12,128]{0,2,1:T(8,128)(2,1)}, u32[]{:S(2)}) copy-start(bf16[512,12,128]{0,2,1:T(8,128)(2,1)} %copy.79) | copy-start | bytes 4718596
  318.7 43.6 %all-to-all-start.6 = ((bf16[8,64,1536]{2,1,0:T(8,128)(2,1)}), bf16[8,64,1536]{2,1,0:T(8,128)(2,1)S(1)}, u32[]{:S(2)}, u32[]{:S(2)}) async-start(bf16[8,64,1536]{2,1,0:T(8,128)(2,1)} %add_convert_fusion), calls=%async_computation.6 | async-start | bytes 3145728 | tf_op jit(solution)/shard_map/all_to_all | solution.py:92
  331.1 33.6 %collective-permute-start = (bf16[64,12288]{1,0:T(8,128)(2,1)}, bf16[64,12288]{1,0:T(8,128)(2,1)}, u32[]{:S(2)}, u32[]{:S(2)}) collective-permute-start(bf16[64,12288]{1,0:T(8,128)(2,1)} %fusion.26), channel_id=1, source_target_pairs={{0,8},{8,16},{16,24},{24,32},{32,40},{40,48},{48,56},{56,64},{64,7... | collective-permute-start | bytes 4718600 | tf_op jit(solution)/shard_map/ppermute | solution.py:20
  362.7 1.4 copy-start.2
  362.9 1.8 copy-start.11
  365.5 1.7 copy-start.5
  367.2 30.0 %all-to-all-start.2 = ((bf16[64,8,1536]{2,0,1:T(8,128)(2,1)}), bf16[64,8,1536]{2,0,1:T(8,128)(2,1)}, u32[]{:S(2)}, u32[]{:S(2)}) async-start(bf16[64,8,1536]{2,0,1:T(8,128)(2,1)} %bitcast.84), calls=%async_computation.2 | async-start | bytes 3145728 | tf_op jit(solution)/shard_map/all_to_all | solution.py:49
  371.7 4.0 copy-start.7
  423.7 8.6 %copy-start.4 = (bf16[1,64,12288]{2,1,0:T(8,128)(2,1)S(1)}, bf16[1,64,12288]{2,1,0:T(8,128)(2,1)}, u32[]{:S(2)}) copy-start(bf16[1,64,12288]{2,1,0:T(8,128)(2,1)} %param.7) | copy-start | bytes 4718596
  427.8 28.4 %all-to-all-start.3 = ((bf16[8,64,1536]{2,1,0:T(8,128)(2,1)}), bf16[8,64,1536]{2,1,0:T(8,128)(2,1)S(1)}, u32[]{:S(2)}, u32[]{:S(2)}) async-start(bf16[8,64,1536]{2,1,0:T(8,128)(2,1)} %all_to_all.73), calls=%async_computation.3 | async-start | bytes 3145728 | tf_op jit(solution)/shard_map/all_to_all | solution.py:56
  456.6 1.4 copy-start.6
where the time goes:
time: 470 us; the launch traced here: 462 us
  waiting for transfers between devices  201 us (43%)
  local copies, waits for them, and re-layouts  85.5 us (18%)
  other arithmetic  67.9 us (14%)
  matrix products  58.2 us (12%)
  starting transfers between devices  48.6 us (10%)
    ppermute x8, waiting for transfers between devices, from_partner(): return lax.ppermute(value, axis, pairs)  103 us
    all_to_all x2, waiting for transfers between devices, forward(): lax.all_to_all(normed, 'tensor', split_axis=1, concat_axis=0, tiled=True)  34.7 us
    all_to_all x1, waiting for transfers between devices, backward(): lax.all_to_all(normed_grad, 'tensor', split_axis=0, concat_axis=1, tiled=...  28.7 us
    all_to_all x2, waiting for transfers between devices, forward(): lax.all_to_all(mixed_out, 'tensor', split_axis=0, concat_axis=1, tiled=True)  20.6 us
    convert_element_type x5, local copies, waits for them, and re-layouts, heads_of(): scaled = (normed.astype(jnp.float32) * feature_gain).astype(jnp.bfloat16)  19 us
    convert_element_type x5, other arithmetic, heads_of(): scaled = (normed.astype(jnp.float32) * feature_gain).astype(jnp.bfloat16)  17.7 us
    sub x2, other arithmetic, softmax_causal(): weights = jnp.exp(scores - largest)  16.4 us
    dot_general x2, matrix products, forward(): jnp.einsum('hij,jhd->ihd', weights, value_heads, preferred_element_type=j...  14.1 us
  transfers between devices with their start and end apart: 16, of which 11 were waited for; matrix products, arithmetic and copies ran while one was open for 36% of the time, Pallas kernels for 0%

commit v1 on v0

--- a/solution.py
+++ b/solution.py
@@ -6,6 +6,12 @@
 HDIM = 128
 epsilon = 1e-05
 masked_score = -1e30
+
+
+def stacked_exchange(block, axis, split, join):
+    cells = jnp.split(block, lax.axis_size(axis), axis=split)
+    received = lax.all_to_all(jnp.stack(cells), axis, 0, 0)
+    return jnp.concatenate(received, axis=join)
 
 
 def from_partner(value, axis, distance):
@@ -89,9 +95,7 @@
         query_grad.reshape(head_shape) * query_gain + key_grad.reshape(head_shape) * key_gain
     )
     normed_grad = (normed_grad + value_grad.reshape(head_shape) * value_gain).astype(jnp.bfloat16)
-    returned = lax.all_to_all(
-        normed_grad, "tensor", split_axis=0, concat_axis=1, tiled=True
-    ).astype(jnp.float32)
+    returned = stacked_exchange(normed_grad, "tensor", 0, 1).astype(jnp.float32)
     inner = jnp.mean(returned * scaled, axis=-1, keepdims=True)
     return (grad_rows.astype(jnp.float32) + factor * (returned - scaled * inner)).astype(
         jnp.bfloat16

time: 470 us -> 452 us (0.962)
  local copies, waits for them, and re-layouts: 85.5 us -> 77.5 us
    mul x2 -> x0, local copies, waits for them, and re-layouts: 10.2 us -> none  [the longest x1 5.1 us: backward(): key_grad = key_grad * HDIM ** (-0.5)]
    unnamed x33 -> x52, local copies, waits for them, and re-layouts: 9.98 us -> 14.7 us
  transfers between devices with their start and end apart: 16 -> 16, of which waited for: 11 -> 12; matrix products, arithmetic and copies ran while one was open for 36% -> 34% of each run, Pallas kernels for 0% -> 0%
where the time goes in v1:
time: 452 us; the launch traced here: 444 us
  waiting for transfers between devices  197 us (44%)
  local copies, waits for them, and re-layouts  77.5 us (17%)
  other arithmetic  66.7 us (15%)
  matrix products  54.5 us (12%)
  starting transfers between devices  47.3 us (10%)
    ppermute x8, waiting for transfers between devices, from_partner(): return lax.ppermute(value, axis, pairs)  103 us
    all_to_all x2, waiting for transfers between devices, forward(): lax.all_to_all(normed, 'tensor', split_axis=1, concat_axis=0, tiled=True)  34.7 us
    all_to_all x1, waiting for transfers between devices, stacked_exchange(): received = lax.all_to_all(jnp.stack(cells), axis, 0, 0)  28.6 us
    all_to_all x2, waiting for transfers between devices, forward(): lax.all_to_all(mixed_out, 'tensor', split_axis=0, concat_axis=1, tiled=True)  21.2 us
    convert_element_type x5, local copies, waits for them, and re-layouts, heads_of(): scaled = (normed.astype(jnp.float32) * feature_gain).astype(jnp.bfloat16)  19.1 us
    convert_element_type x5, other arithmetic, heads_of(): scaled = (normed.astype(jnp.float32) * feature_gain).astype(jnp.bfloat16)  17.9 us
    sub x2, other arithmetic, softmax_causal(): weights = jnp.exp(scores - largest)  16.4 us
    unnamed x52, local copies, waits for them, and re-layouts  14.7 us
  transfers between devices with their start and end apart: 16, of which 12 were waited for; matrix products, arithmetic and copies ran while one was open for 34% of the time, Pallas kernels for 0%

profile of v1, /device:TPU:0, one launch (start us, length us, event | category | flops | bytes accessed | tf_op | source)
XLA Modules:
  0.0 444.3 jit_solution(747477331206184728)
XLA Ops:
  0.7 3.6 collective-permute-done.5
  4.3 1.7 collective-permute-start.6
  6.0 34.7 %collective-permute-done.6 = bf16[64,12288]{1,0:T(8,128)(2,1)S(1)} collective-permute-done((bf16[64,12288]{1,0:T(8,128)(2,1)S(1)}, bf16[64,12288]{1,0:T(8,128)(2,1)S(1)}, u32[]{:S(2)}, u32[]{:S(2)}) %collective-permute-start.6) | collective-permute-done | bytes 1572896 | tf_op jit(solution)/shard_map/ppermute | solution.py:20
  40.8 3.3 collective-permute-start.7
  44.8 34.9 %collective-permute-done.7 = bf16[64,12288]{1,0:T(8,128)(2,1)} collective-permute-done((bf16[64,12288]{1,0:T(8,128)(2,1)S(1)}, bf16[64,12288]{1,0:T(8,128)(2,1)}, u32[]{:S(2)}, u32[]{:S(2)}) %collective-permute-start.7) | collective-permute-done | bytes 1572896 | tf_op jit(solution)/shard_map/ppermute | solution.py:20
  79.6 2.0 collective-permute-start.8
  81.7 1.9 copy.156
  83.6 1.6 copy.132
  85.2 7.3 %all-to-all-start.5 = ((bf16[64,8,1536]{2,0,1:T(8,128)(2,1)}), bf16[64,8,1536]{2,0,1:T(8,128)(2,1)}, u32[]{:S(2)}, u32[]{:S(2)}) async-start(bf16[64,8,1536]{2,0,1:T(8,128)(2,1)} %copy.132), calls=%async_computation.5 | async-start | bytes 3145728 | tf_op jit(solution)/shard_map/all_to_all | solution.py:71
  93.5 2.9 fusion.36
  96.4 15.8 %collective-permute-done.2 = bf16[64,12288]{1,0:T(8,128)(2,1)} collective-permute-done((bf16[64,12288]{1,0:T(8,128)(2,1)}, bf16[64,12288]{1,0:T(8,128)(2,1)}, u32[]{:S(2)}, u32[]{:S(2)}) %collective-permute-start.2) | collective-permute-done | bytes 1572896 | tf_op jit(solution)/shard_map/ppermute | solution.py:20
  112.1 1.8 collective-permute-start.3
  114.0 14.0 %collective-permute-done.8 = bf16[64,12288]{1,0:T(8,128)(2,1)S(1)} collective-permute-done((bf16[64,12288]{1,0:T(8,128)(2,1)}, bf16[64,12288]{1,0:T(8,128)(2,1)S(1)}, u32[]{:S(2)}, u32[]{:S(2)}) %collective-permute-start.8) | collective-permute-done | bytes 1572896 | tf_op jit(solution)/shard_map/ppermute | solution.py:20
  128.3 5.1 %all-to-all-done.5 = bf16[64,8,1536]{2,0,1:T(8,128)(2,1)} async-done(((bf16[64,8,1536]{2,0,1:T(8,128)(2,1)}), bf16[64,8,1536]{2,0,1:T(8,128)(2,1)}, u32[]{:S(2)}, u32[]{:S(2)}) %all-to-all-start.5) | async-done | bytes 1572896 | tf_op jit(solution)/shard_map/all_to_all | solution.py:71
  133.4 4.3 all-to-all-start
  139.4 17.0 %all-to-all-done = bf16[64,8,1536]{2,0,1:T(8,128)(2,1)} async-done(((bf16[64,8,1536]{2,0,1:T(8,128)(2,1)}), bf16[64,8,1536]{2,0,1:T(8,128)(2,1)}, u32[]{:S(2)}, u32[]{:S(2)}) %all-to-all-start) | async-done | bytes 1572896 | tf_op jit(solution)/shard_map/all_to_all | solution.py:55
  156.4 4.1 all-to-all-start.4
  160.7 4.0 reshape.178
  164.6 4.3 copy.142
  168.9 3.5 convert_bitcast_fusion.6
  172.4 4.6 %reshape.183 = f32[512,12,128]{2,1,0:T(8,128)} reshape(f32[8,64,1536]{2,1,0:T(8,128)} %convert_bitcast_fusion.6) | data formatting | bytes 6291456 | tf_op jit(solution)/shard_map/convert_element_type | solution.py:36
  177.5 4.3 all-to-all-done.4
  181.9 2.1 convert_bitcast_fusion.3
  184.0 4.7 %reshape.189 = f32[512,12,128]{2,1,0:T(8,128)} reshape(f32[8,64,1536]{2,1,0:T(8,128)} %convert_bitcast_fusion.3) | data formatting | bytes 6291456 | tf_op jit(solution)/shard_map/convert_element_type | solution.py:36
  188.6 7.3 %multiply_convert_fusion.8 = (bf16[512,12,128]{2,1,0:T(8,128)(2,1)}, bf16[512,12,128]{2,1,0:T(8,128)(2,1)}, bf16[512,12,128]{2,1,0:T(8,128)(2,1)}, bf16[512,12,1...) fusion(f32[512,12,128]{2,1,0:T(8,128)} %reshape.183, f32[12,128]{1,0:T(8,128)S(1)} %bitcast.135, ...), kind=kLoop, calls=%fused_computation.44 | loop fusion | flops 9437184 | bytes 15747072 | tf_op jit(solution)/shard_map/convert_element_type | solution.py:36
  195.9 3.3 copy.135
  199.2 4.3 copy.138
  203.4 10.5 %fusion.75 = (f32[12,512]{1,0:T(8,128)S(1)}, f32[12,512,512]{1,2,0:T(8,128)}) fusion(pred[512,512]{0,1:T(8,128)(4,1)S(1)} %iota_compare_fusion, bf16[512,12,128]{0,2,1:T(8,128)(2,1)} %copy.138, bf16[512,12,128]{0,2,1:T(8,128)(2,1)S(1)} %copy.135), kind=kOutput, calls=%fused_computation.125 | convolution fusion | flops 817889792 | bytes 16015360 | tf_op jit(solution)/shard_map/sub | solution.py:48
  214.0 9.0 %fusion.9 = f32[12,512,128]{1,2,0:T(8,128)} fusion(bf16[512,12,128]{0,2,1:T(8,128)(2,1)} %copy.142, f32[12,512,512]{1,2,0:T(8,128)} %get-tuple-element.25, f32[12,512]{1,0:T(8,128)S(1)} %get-tuple-element.24), kind=kOutput, calls=%fused_computation.19 | convolution fusion | flops 811597824 | bytes 17326080 | tf_op jit(solution)/shard_map/hij,ihd->jhd/dot_general | solution.py:79
  223.0 11.3 %fusion.3 = (f32[12,512]{1,0:T(8,128)S(1)}, f32[12,512,512]{2,1,0:T(8,128)}) fusion(f32[12,512,512]{1,2,0:T(8,128)} %get-tuple-element.25, f32[12,512]{1,0:T(8,128)S(1)} %get-tuple-element.24, bf16[512,12,128]{0,2,1:T(8,128)(2,1)S(1)} %copy-done.14, bf16[512,12,128]{2,1,0:T(8,128)(2,1)S(1)} %copy-done.12), kind=kOutput, calls=%fused_computation.5 | convolution fusion | flops 814737408 | bytes 28360704 | tf_op jit(solution)/shard_map/ihd,jhd->hij/dot_general | solution.py:82
  235.6 7.0 %fusion.5 = bf16[12,512,512]{1,2,0:T(8,128)(2,1)S(1)} fusion(f32[12,512,512]{2,1,0:T(8,128)} %get-tuple-element.27, f32[12,512]{1,0:T(8,128)S(1)} %get-tuple-element.26, f32[12,512,512]{1,2,0:T(8,128)S(1)} %bitcast.124, f32[12,512]{1,0:T(8,128)S(1)} %get-tuple-element.24), kind=kLoop, calls=%fused_computation.7 | loop fusion | flops 12582912 | bytes 31506432 | tf_op jit(solution)/shard_map/convert_element_type | solution.py:86
  242.7 3.8 convolution_multiply_fusion
  246.5 2.7 convolution_multiply_fusion.1
  249.2 1.9 fusion.48
  251.1 8.2 %fusion.73 = (f32[12,512]{1,0:T(8,128)S(1)}, f32[12,512,512]{1,2,0:T(8,128)}) fusion(f32[12,512,512]{1,2,0:T(8,128)S(1)} %fusion.48, pred[512,512]{0,1:T(8,128)(4,1)S(1)} %iota_compare_fusion), kind=kOutput, calls=%fused_computation.123 | output fusion | flops 18874880 | bytes 25452544 | tf_op jit(solution)/shard_map/sub | solution.py:48
  259.3 7.3 %fusion.51 = bf16[512,12,128]{0,2,1:T(8,128)(2,1)} fusion(f32[12,512,512]{1,2,0:T(8,128)} %get-tuple-element.21, f32[12,512]{1,0:T(8,128)S(1)} %get-tuple-element.20, bf16[512,12,128]{2,1,0:T(8,128)(2,1)S(1)} %copy-done.11), kind=kOutput, calls=%fused_computation.93 | convolution fusion | flops 812384256 | bytes 15753216 | tf_op jit(solution)/shard_map/hij,jhd->ihd/dot_general | solution.py:60
  266.5 4.4 copy.119
  270.9 4.0 all_to_all.64
  274.9 3.6 all-to-all-start.1
  278.5 3.6 copy.143
  282.0 3.5 copy.137
  285.6 3.5 copy.140
  289.1 4.9 %add_convert_fusion = bf16[512,1536]{1,0:T(8,128)(2,1)S(1)} fusion(f32[512,1536]{1,0:T(8,128)} %copy.143, f32[512,1536]{1,0:T(8,128)} %copy.140, f32[512,1536]{1,0:T(8,128)} %copy.137, f32[1536]{0:T(1024)S(1)} %reduce, f32[1536]{0:T(1024)S(1)} %reduce.2, f32[1536]{0:T(1024)S(1)} %reduce.1), kind=kLoop, calls=%fused_computation.72 | loop fusion | flops 4718592 | bytes 11028480 | tf_op jit(solution)/shard_map/convert_element_type | solution.py:97
  301.3 6.5 %all-to-all-start.6 = ((bf16[8,64,1536]{2,1,0:T(8,128)(2,1)}), bf16[8,64,1536]{2,1,0:T(8,128)(2,1)S(1)}, u32[]{:S(2)}, u32[]{:S(2)}) async-start(bf16[8,64,1536]{2,1,0:T(8,128)(2,1)} %fusion.59), calls=%async_computation.6 | async-start | bytes 3145728 | tf_op jit(solution)/shard_map/all_to_all | solution.py:13
  307.8 3.5 convert_bitcast_fusion
  313.1 2.4 collective-permute-start
  315.5 28.6 %all-to-all-done.6 = bf16[8,64,1536]{2,1,0:T(8,128)(2,1)S(1)} async-done(((bf16[8,64,1536]{2,1,0:T(8,128)(2,1)}), bf16[8,64,1536]{2,1,0:T(8,128)(2,1)S(1)}, u32[]{:S(2)}, u32[]{:S(2)}) %all-to-all-start.6) | async-done | bytes 1572896 | tf_op jit(solution)/shard_map/all_to_all | solution.py:13
  349.1 4.5 %all-to-all-start.2 = ((bf16[64,8,1536]{2,0,1:T(8,128)(2,1)}), bf16[64,8,1536]{2,0,1:T(8,128)(2,1)}, u32[]{:S(2)}, u32[]{:S(2)}) async-start(bf16[64,8,1536]{2,0,1:T(8,128)(2,1)} %bitcast.125), calls=%async_computation.2 | async-start | bytes 3145728 | tf_op jit(solution)/shard_map/all_to_all | solution.py:55
  353.6 4.0 fusion.40
  357.6 1.8 copy.120
  359.5 1.9 reshape.184
  361.4 17.8 %all-to-all-done.2 = bf16[64,8,1536]{2,0,1:T(8,128)(2,1)} async-done(((bf16[64,8,1536]{2,0,1:T(8,128)(2,1)}), bf16[64,8,1536]{2,0,1:T(8,128)(2,1)}, u32[]{:S(2)}, u32[]{:S(2)}) %all-to-all-start.2) | async-done | bytes 1572896 | tf_op jit(solution)/shard_map/all_to_all | solution.py:55
  379.2 1.8 convert_bitcast_fusion.5
  381.0 2.2 reshape.186
  383.2 3.2 multiply_convert_fusion.5
  386.4 1.9 fusion.44
  388.3 8.2 %fusion.74 = (f32[12,512]{1,0:T(8,128)S(1)}, f32[12,512,512]{1,2,0:T(8,128)}) fusion(f32[12,512,512]{1,2,0:T(8,128)S(1)} %fusion.44, pred[512,512]{0,1:T(8,128)(4,1)S(1)} %iota_compare_fusion), kind=kOutput, calls=%fused_computation.124 | output fusion | flops 18874880 | bytes 25452544 | tf_op jit(solution)/shard_map/sub | solution.py:48
  396.5 6.1 %fusion.54 = bf16[512,12,128]{0,2,1:T(8,128)(2,1)S(1)} fusion(f32[12,512,512]{1,2,0:T(8,128)} %get-tuple-element.23, f32[12,512]{1,0:T(8,128)S(1)} %get-tuple-element.22, bf16[512,12,128]{2,1,0:T(8,128)(2,1)S(1)} %get-tuple-element.9), kind=kOutput, calls=%fused_computation.94 | convolution fusion | flops 812384256 | bytes 15753216 | tf_op jit(solution)/shard_map/hij,jhd->ihd/dot_general | solution.py:60
  402.7 3.0 copy.127
  405.7 4.1 all_to_all.68
  409.7 4.5 %all-to-all-start.3 = ((bf16[8,64,1536]{2,1,0:T(8,128)(2,1)}), bf16[8,64,1536]{2,1,0:T(8,128)(2,1)S(1)}, u32[]{:S(2)}, u32[]{:S(2)}) async-start(bf16[8,64,1536]{2,1,0:T(8,128)(2,1)} %all_to_all.68), calls=%async_computation.3 | async-start | bytes 3145728 | tf_op jit(solution)/shard_map/all_to_all | solution.py:62
  414.2 3.3 add_convert_fusion.1
  417.5 20.6 %all-to-all-done.3 = bf16[8,64,1536]{2,1,0:T(8,128)(2,1)S(1)} async-done(((bf16[8,64,1536]{2,1,0:T(8,128)(2,1)}), bf16[8,64,1536]{2,1,0:T(8,128)(2,1)S(1)}, u32[]{:S(2)}, u32[]{:S(2)}) %all-to-all-start.3) | async-done | bytes 1572896 | tf_op jit(solution)/shard_map/all_to_all | solution.py:62
  441.3 2.7 copy.192
  (84 shorter events, 22.9 us)
Async XLA Ops:
  0.6 3.7 collective-permute-start.5
  4.3 36.4 %collective-permute-start.6 = (bf16[64,12288]{1,0:T(8,128)(2,1)S(1)}, bf16[64,12288]{1,0:T(8,128)(2,1)S(1)}, u32[]{:S(2)}, u32[]{:S(2)}) collective-permute-start(bf16[64,12288]{1,0:T(8,128)(2,1)S(1)} %collective-permute-done.5), channel_id=1, source_target_pairs={{0,16},{8,24},{16,0},{24,8},{32,48},{40,56},{48,32},{56,40},{64,80... | collective-permute-start | bytes 4718600 | tf_op jit(solution)/shard_map/ppermute | solution.py:20
  6.0 38.1 %collective-permute-start.1 = (bf16[64,12288]{1,0:T(8,128)(2,1)}, bf16[64,12288]{1,0:T(8,128)(2,1)}, u32[]{:S(2)}, u32[]{:S(2)}) collective-permute-start(bf16[64,12288]{1,0:T(8,128)(2,1)} %bitcast.116), channel_id=1, source_target_pairs={{0,8},{8,0},{16,24},{24,16},{32,40},{40,32},{48,56},{56,48},{64,72... | collective-permute-start | bytes 4718600 | tf_op jit(solution)/shard_map/ppermute | solution.py:20
  40.8 38.9 %collective-permute-start.7 = (bf16[64,12288]{1,0:T(8,128)(2,1)S(1)}, bf16[64,12288]{1,0:T(8,128)(2,1)}, u32[]{:S(2)}, u32[]{:S(2)}) collective-permute-start(bf16[64,12288]{1,0:T(8,128)(2,1)S(1)} %collective-permute-done.6), channel_id=1, source_target_pairs={{0,32},{8,40},{16,48},{24,56},{32,0},{40,8},{48,16},{56,24},{64,96... | collective-permute-start | bytes 4718600 | tf_op jit(solution)/shard_map/ppermute | solution.py:20
  44.1 68.0 %collective-permute-start.2 = (bf16[64,12288]{1,0:T(8,128)(2,1)}, bf16[64,12288]{1,0:T(8,128)(2,1)}, u32[]{:S(2)}, u32[]{:S(2)}) collective-permute-start(bf16[64,12288]{1,0:T(8,128)(2,1)} %collective-permute-done.1), channel_id=1, source_target_pairs={{0,16},{8,24},{16,0},{24,8},{32,48},{40,56},{48,32},{56,40},{64,80... | collective-permute-start | bytes 4718600 | tf_op jit(solution)/shard_map/ppermute | solution.py:20
  79.6 48.3 %collective-permute-start.8 = (bf16[64,12288]{1,0:T(8,128)(2,1)}, bf16[64,12288]{1,0:T(8,128)(2,1)S(1)}, u32[]{:S(2)}, u32[]{:S(2)}) collective-permute-start(bf16[64,12288]{1,0:T(8,128)(2,1)} %collective-permute-done.7), channel_id=1, source_target_pairs={{0,64},{8,72},{16,80},{24,88},{32,96},{40,104},{48,112},{56,120},{... | collective-permute-start | bytes 4718600 | tf_op jit(solution)/shard_map/ppermute | solution.py:20
  83.6 8.9 %copy-start.2 = (bf16[1,64,12288]{2,1,0:T(8,128)(2,1)S(1)}, bf16[1,64,12288]{2,1,0:T(8,128)(2,1)}, u32[]{:S(2)}) copy-start(bf16[1,64,12288]{2,1,0:T(8,128)(2,1)} %param.7) | copy-start | bytes 4718596
  85.2 48.2 %all-to-all-start.5 = ((bf16[64,8,1536]{2,0,1:T(8,128)(2,1)}), bf16[64,8,1536]{2,0,1:T(8,128)(2,1)}, u32[]{:S(2)}, u32[]{:S(2)}) async-start(bf16[64,8,1536]{2,0,1:T(8,128)(2,1)} %copy.132), calls=%async_computation.5 | async-start | bytes 3145728 | tf_op jit(solution)/shard_map/all_to_all | solution.py:71
  112.1 64.9 %collective-permute-start.3 = (bf16[64,12288]{1,0:T(8,128)(2,1)}, bf16[64,12288]{1,0:T(8,128)(2,1)}, u32[]{:S(2)}, u32[]{:S(2)}) collective-permute-start(bf16[64,12288]{1,0:T(8,128)(2,1)} %collective-permute-done.2), channel_id=1, source_target_pairs={{0,32},{8,40},{16,48},{24,56},{32,0},{40,8},{48,16},{56,24},{64,96... | collective-permute-start | bytes 4718600 | tf_op jit(solution)/shard_map/ppermute | solution.py:20
  127.9 10.2 %copy-start = (bf16[64,12288]{1,0:T(8,128)(2,1)}, bf16[64,12288]{1,0:T(8,128)(2,1)S(1)}, u32[]{:S(2)}) copy-start(bf16[64,12288]{1,0:T(8,128)(2,1)S(1)} %collective-permute-done.8) | copy-start | bytes 4718596
  133.4 22.9 %all-to-all-start = ((bf16[64,8,1536]{2,0,1:T(8,128)(2,1)}), bf16[64,8,1536]{2,0,1:T(8,128)(2,1)}, u32[]{:S(2)}, u32[]{:S(2)}) async-start(bf16[64,8,1536]{2,0,1:T(8,128)(2,1)} %fusion.36), calls=%async_computation | async-start | bytes 3145728 | tf_op jit(solution)/shard_map/all_to_all | solution.py:55
  138.1 22.4 %copy-start.15 = (f32[1,1536]{1,0:T(1,128)S(1)}, f32[1,1536]{1,0:T(1,128)}, u32[]{:S(2)}) copy-start(f32[1,1536]{1,0:T(1,128)} %param.11) | copy-start | bytes 18436
  138.1 22.4 %copy-start.16 = (f32[1,1536]{1,0:T(1,128)S(1)}, f32[1,1536]{1,0:T(1,128)}, u32[]{:S(2)}) copy-start(f32[1,1536]{1,0:T(1,128)} %param.12) | copy-start | bytes 18436
  138.1 22.4 %copy-start.17 = (f32[1,1536]{1,0:T(1,128)S(1)}, f32[1,1536]{1,0:T(1,128)}, u32[]{:S(2)}) copy-start(f32[1,1536]{1,0:T(1,128)} %param.13) | copy-start | bytes 18436
  156.4 25.5 %all-to-all-start.4 = ((bf16[64,8,1536]{2,0,1:T(8,128)(2,1)}), bf16[64,8,1536]{2,0,1:T(8,128)(2,1)S(1)}, u32[]{:S(2)}, u32[]{:S(2)}) async-start(bf16[64,8,1536]{2,0,1:T(8,128)(2,1)} %bitcast.112), calls=%async_computation.4 | async-start | bytes 3145728 | tf_op jit(solution)/shard_map/all_to_all | solution.py:70
  177.0 138.5 %collective-permute-start.4 = (bf16[64,12288]{1,0:T(8,128)(2,1)}, bf16[64,12288]{1,0:T(8,128)(2,1)}, u32[]{:S(2)}, u32[]{:S(2)}) collective-permute-start(bf16[64,12288]{1,0:T(8,128)(2,1)} %collective-permute-done.3), channel_id=1, source_target_pairs={{0,64},{8,72},{16,80},{24,88},{32,96},{40,104},{48,112},{56,120},{... | collective-permute-start | bytes 4718600 | tf_op jit(solution)/shard_map/ppermute | solution.py:20
  214.0 9.0 %copy-start.12 = (bf16[512,12,128]{2,1,0:T(8,128)(2,1)S(1)}, bf16[512,12,128]{2,1,0:T(8,128)(2,1)}, u32[]{:S(2)}) copy-start(bf16[512,12,128]{2,1,0:T(8,128)(2,1)} %get-tuple-element.19) | copy-start | bytes 4718596
  214.0 9.0 %copy-start.14 = (bf16[512,12,128]{0,2,1:T(8,128)(2,1)S(1)}, bf16[512,12,128]{0,2,1:T(8,128)(2,1)}, u32[]{:S(2)}) copy-start(bf16[512,12,128]{0,2,1:T(8,128)(2,1)} %copy.142) | copy-start | bytes 4718596
  223.0 11.3 %slice-start = ((s8[12582912]{0:T(1024)(128)(4,1)}), s8[4194304]{0:T(1024)(128)(4,1)S(1)}, s32[]{:S(2)}) async-start(s8[12582912]{0:T(1024)(128)(4,1)} %bitcast.123), calls=%async_computation.7 | async-start | bytes 8388608
  223.0 11.3 %slice-start.1 = ((s8[12582912]{0:T(1024)(128)(4,1)}), s8[4194304]{0:T(1024)(128)(4,1)S(1)}, s32[]{:S(2)}) async-start(s8[12582912]{0:T(1024)(128)(4,1)} %bitcast.123), calls=%async_computation.8 | async-start | bytes 8388608
  223.0 12.6 %slice-start.2 = ((s8[12582912]{0:T(1024)(128)(4,1)}), s8[4194304]{0:T(1024)(128)(4,1)S(1)}, s32[]{:S(2)}) async-start(s8[12582912]{0:T(1024)(128)(4,1)} %bitcast.123), calls=%async_computation.9 | async-start | bytes 8388608
  235.6 7.1 %copy-start.9 = (bf16[512,12,128]{0,2,1:T(8,128)(2,1)S(1)}, bf16[512,12,128]{0,2,1:T(8,128)(2,1)}, u32[]{:S(2)}) copy-start(bf16[512,12,128]{0,2,1:T(8,128)(2,1)} %copy.138) | copy-start | bytes 4718596
  246.5 2.7 copy-start.7
  246.5 2.7 copy-start.8
  251.0 8.2 %copy-start.11 = (bf16[512,12,128]{2,1,0:T(8,128)(2,1)S(1)}, bf16[512,12,128]{2,1,0:T(8,128)(2,1)}, u32[]{:S(2)}) copy-start(bf16[512,12,128]{2,1,0:T(8,128)(2,1)} %get-tuple-element.12) | copy-start | bytes 4718596
  274.9 25.3 %all-to-all-start.1 = ((bf16[8,64,1536]{2,1,0:T(8,128)(2,1)}), bf16[8,64,1536]{2,1,0:T(8,128)(2,1)S(1)}, u32[]{:S(2)}, u32[]{:S(2)}) async-start(bf16[8,64,1536]{2,1,0:T(8,128)(2,1)} %all_to_all.64), calls=%async_computation.1 | async-start | bytes 3145728 | tf_op jit(solution)/shard_map/all_to_all | solution.py:62
  300.2 1.1 copy-start.10
  301.3 42.8 %all-to-all-start.6 = ((bf16[8,64,1536]{2,1,0:T(8,128)(2,1)}), bf16[8,64,1536]{2,1,0:T(8,128)(2,1)S(1)}, u32[]{:S(2)}, u32[]{:S(2)}) async-start(bf16[8,64,1536]{2,1,0:T(8,128)(2,1)} %fusion.59), calls=%async_computation.6 | async-start | bytes 3145728 | tf_op jit(solution)/shard_map/all_to_all | solution.py:13
  313.1 33.6 %collective-permute-start = (bf16[64,12288]{1,0:T(8,128)(2,1)}, bf16[64,12288]{1,0:T(8,128)(2,1)}, u32[]{:S(2)}, u32[]{:S(2)}) collective-permute-start(bf16[64,12288]{1,0:T(8,128)(2,1)} %fusion.26), channel_id=1, source_target_pairs={{0,8},{8,16},{16,24},{24,32},{32,40},{40,48},{48,56},{56,64},{64,7... | collective-permute-start | bytes 4718600 | tf_op jit(solution)/shard_map/ppermute | solution.py:26
  344.6 1.4 copy-start.1
  344.8 1.8 copy-start.13
  347.4 1.7 copy-start.4
  349.1 30.1 %all-to-all-start.2 = ((bf16[64,8,1536]{2,0,1:T(8,128)(2,1)}), bf16[64,8,1536]{2,0,1:T(8,128)(2,1)}, u32[]{:S(2)}, u32[]{:S(2)}) async-start(bf16[64,8,1536]{2,0,1:T(8,128)(2,1)} %bitcast.125), calls=%async_computation.2 | async-start | bytes 3145728 | tf_op jit(solution)/shard_map/all_to_all | solution.py:55
  353.6 4.0 copy-start.6
  405.7 8.5 %copy-start.3 = (bf16[1,64,12288]{2,1,0:T(8,128)(2,1)S(1)}, bf16[1,64,12288]{2,1,0:T(8,128)(2,1)}, u32[]{:S(2)}) copy-start(bf16[1,64,12288]{2,1,0:T(8,128)(2,1)} %param.7) | copy-start | bytes 4718596
  409.7 28.3 %all-to-all-start.3 = ((bf16[8,64,1536]{2,1,0:T(8,128)(2,1)}), bf16[8,64,1536]{2,1,0:T(8,128)(2,1)S(1)}, u32[]{:S(2)}, u32[]{:S(2)}) async-start(bf16[8,64,1536]{2,1,0:T(8,128)(2,1)} %all_to_all.68), calls=%async_computation.3 | async-start | bytes 3145728 | tf_op jit(solution)/shard_map/all_to_all | solution.py:62
  438.5 1.4 copy-start.5
